TPU v7x, 32 devices: a whole 2x2x4 slice. The times are simulated.
32 devices in a mesh: seq: 4 (over x, core), mp: 8 (over z, y).
Axes of the slice: x: 2, y: 2, z: 4, core: 2. Of those that a mesh axis runs over, the one named last changes fastest.
Arguments:
- queries: bfloat16 [1024, 4096], P('seq', 'mp'), may hold values from -15 to 15
- keys_values: bfloat16 [2, 1024, 4096], P(None, 'seq', 'mp'), may hold values from -6 to 6
- residual: bfloat16 [1024, 4096], P('seq', 'mp'), may hold values from -6 to 6
- cotangent: bfloat16 [1024, 4096], P('seq', 'mp'), may hold values from -6 to 6
- out_weight: bfloat16 [2, 4096, 4096], P(None, 'mp'), may hold values from -0.09375 to 0.09375
- kv_weight: bfloat16 [2, 4096, 4096], P(None, None, 'mp'), may hold values from -0.09375 to 0.09375
- bounds: int32 [2, 1024], replicated, may hold values from 0 to 767, as said below
- windows: int32 [64], P('mp'), may hold values from 1 to 127, as said below
Outputs:
- states_out: bfloat16 [1024, 4096], P('seq', 'mp')
- grad_states: bfloat16 [1024, 4096], P('seq', 'mp')
Inputs may be any that keep to these rules, and one draw needn't show every extreme that they name: The encoder rows form 4 documents, each a run of consecutive positions; an encoder token's bounds are its own document's first and last position. The last document begins among the last 255 encoder positions. Decoder tokens belong to documents in reverse order, the first decoder token to the last document (other documents may have none), and carry that document's encoder bounds. `windows`: some head reaches exactly 127.
All inputs are finite; a program needn't handle non-finite values.
Results may differ from a plain program's by a relative error of at most 0.038.
Values may be sent and summed in bfloat16 or wider, within the bound.
A program may use at most 64 MiB of HBM per device.

v0:
```python
import jax
import jax.numpy as jnp
from jax import lax
from jax.sharding import PartitionSpec as P

HD = 64
WIN = 127


def with_halo(cells, sides, width):
    for axis, dim in sides:
        count = lax.axis_size(axis)
        ends = count - 1
        head = lax.slice_in_dim(cells, 0, width, axis=dim)
        tail = lax.slice_in_dim(cells, cells.shape[dim] - width, cells.shape[dim], axis=dim)
        cells = jnp.concatenate(
            [
                lax.ppermute(tail, axis, [(i, (i + 1) % count) for i in range(ends)]),
                cells,
                lax.ppermute(head, axis, [((i + 1) % count, i) for i in range(ends)]),
            ],
            axis=dim,
        )
    return cells


def softmax_masked(scores, permitted):
    masked_scores = jnp.where(permitted, scores, -jnp.inf)
    row_top = jnp.max(masked_scores, axis=-1, keepdims=True)
    exp_scores = jnp.exp(masked_scores - row_top)
    return exp_scores / jnp.sum(exp_scores, axis=-1, keepdims=True)


def shards(queries, keys_values, residual, cotangent, out_weight, kv_weight, bounds, windows):
    row_count = queries.shape[0]
    col_count = queries.shape[1]
    head_count = col_count // HD
    slab_count = lax.axis_size("seq")
    enc_slabs = 3 * slab_count // 4
    dec_slabs = slab_count - enc_slabs
    enc_tokens = enc_slabs * row_count
    token_count = slab_count * row_count
    dec_tokens = token_count - enc_tokens
    slab_index = lax.axis_index("seq")
    is_enc = slab_index < enc_slabs
    score_scale = HD ** (-0.5)
    own_pos = slab_index * row_count + jnp.arange(row_count, dtype=jnp.int32)
    own_first = lax.dynamic_slice_in_dim(bounds[0], slab_index * row_count, row_count)
    own_last = lax.dynamic_slice_in_dim(bounds[1], slab_index * row_count, row_count)
    query_heads = queries.reshape(row_count, head_count, HD)
    slice_cols = residual.shape[1]
    res_full, cot_full = (
        lax.all_gather(residual, "mp", axis=1, tiled=True),
        lax.all_gather(cotangent, "mp", axis=1, tiled=True),
    )
    model_width = cot_full.shape[1]
    rim_keys = with_halo(keys_values, (("seq", 1),), WIN)

    def local_part():
        span_count = rim_keys.shape[1]
        key_pos = slab_index * row_count - WIN + jnp.arange(span_count, dtype=jnp.int32)
        key_heads = rim_keys[0].reshape(span_count, head_count, HD)
        value_heads = rim_keys[1].reshape(span_count, head_count, HD)
        scores = (
            jnp.einsum("qhd,khd->hqk", query_heads, key_heads, preferred_element_type=jnp.float32)
            * score_scale
        )
        in_document = (key_pos[None, :] >= own_first[:, None]) & (
            key_pos[None, :] <= own_last[:, None]
        )
        distance = jnp.abs(own_pos[:, None] - key_pos[None, :])
        permitted = in_document[None] & (distance[None] <= windows[:, None, None])
        rounded = softmax_masked(scores, permitted).astype(jnp.bfloat16)
        context = jnp.einsum(
            "hqk,khd->qhd", rounded, value_heads, preferred_element_type=jnp.float32
        ).astype(jnp.bfloat16)
        return jnp.dot(
            context.reshape(row_count, col_count), out_weight[0], preferred_element_type=jnp.float32
        )

    head_partial = lax.cond(
        is_enc, local_part, lambda: jnp.zeros((row_count, model_width), jnp.float32)
    )
    attn_sum = lax.psum(head_partial.astype(jnp.bfloat16), "mp").astype(jnp.float32)
    hidden_full = (res_full.astype(jnp.float32) + attn_sum).astype(jnp.bfloat16)
    encoder_out = lax.dynamic_slice_in_dim(
        hidden_full, lax.axis_index("mp") * slice_cols, slice_cols, 1
    )

    def project_keys():
        key_proj = jnp.dot(hidden_full, kv_weight[0], preferred_element_type=jnp.float32).astype(
            jnp.bfloat16
        )
        value_proj = jnp.dot(hidden_full, kv_weight[1], preferred_element_type=jnp.float32).astype(
            jnp.bfloat16
        )
        return jnp.stack([key_proj, value_proj])

    cross_kv = lax.cond(
        is_enc, project_keys, lambda: jnp.zeros((2, row_count, col_count), jnp.bfloat16)
    )

    def context_gradient():
        return lax.dot_general(
            cot_full, out_weight[1], (((1,), (1,)), ((), ())), preferred_element_type=jnp.float32
        ).astype(jnp.bfloat16)

    dec_queries = lax.all_gather(queries, "seq", axis=0, tiled=True)[enc_tokens:]
    dec_heads = dec_queries.reshape(dec_tokens, head_count, HD)
    dec_first = bounds[0, enc_tokens:]
    dec_last = bounds[1, enc_tokens:]
    in_document = (own_pos[None, :] >= dec_first[:, None]) & (own_pos[None, :] <= dec_last[:, None])
    key_heads = cross_kv[0].reshape(row_count, head_count, HD)
    value_heads = cross_kv[1].reshape(row_count, head_count, HD)
    scores = (
        jnp.einsum("qhd,khd->hqk", dec_heads, key_heads, preferred_element_type=jnp.float32)
        * score_scale
    )
    masked_scores = jnp.where(in_document[None], scores, -jnp.inf)
    row_top = lax.pmax(jnp.max(masked_scores, axis=2), "seq")
    exp_scores = jnp.exp(masked_scores - row_top[:, :, None])
    row_total = lax.psum(jnp.sum(exp_scores, axis=2), "seq")
    weights = exp_scores / row_total[:, :, None]
    rounded = weights.astype(jnp.bfloat16)
    partial_ctx = jnp.einsum(
        "hqk,khd->qhd", rounded, value_heads, preferred_element_type=jnp.float32
    ).reshape(dec_tokens, col_count)
    context_all = lax.psum(partial_ctx.astype(jnp.bfloat16), "seq")
    dec_offset = jnp.maximum(slab_index - enc_slabs, 0) * row_count
    context = lax.dynamic_slice_in_dim(context_all, dec_offset, row_count, 0)
    out_part = lax.cond(
        is_enc,
        lambda: jnp.zeros((row_count, model_width), jnp.float32),
        lambda: jnp.dot(context, out_weight[1], preferred_element_type=jnp.float32),
    )
    grad_own = lax.cond(
        is_enc, lambda: jnp.zeros((row_count, col_count), jnp.bfloat16), context_gradient
    )
    grad_all = lax.all_gather(grad_own, "seq", axis=0, tiled=True)[enc_tokens:]
    grad_heads = grad_all.reshape(dec_tokens, head_count, HD)
    row_dots = jnp.einsum(
        "qhd,qhd->hq",
        grad_heads,
        context_all.reshape(dec_tokens, head_count, HD),
        preferred_element_type=jnp.float32,
    )
    prob_grad = jnp.einsum(
        "qhd,khd->hqk", grad_heads, value_heads, preferred_element_type=jnp.float32
    )
    score_grad = (weights * (prob_grad - row_dots[:, :, None])).astype(jnp.bfloat16)
    grad_blocks = score_grad.reshape(head_count, dec_slabs, row_count, row_count)
    prob_blocks = rounded.reshape(head_count, dec_slabs, row_count, row_count)
    query_blocks = dec_heads.reshape(dec_slabs, row_count, head_count, HD)
    grad_rows = grad_heads.reshape(dec_slabs, row_count, head_count, HD)
    key_parts = (
        score_scale
        * jnp.einsum(
            "hsqk,sqhd->skhd", grad_blocks, query_blocks, preferred_element_type=jnp.float32
        )
    ).astype(jnp.bfloat16)
    value_parts = jnp.einsum(
        "hsqk,sqhd->skhd", prob_blocks, grad_rows, preferred_element_type=jnp.float32
    ).astype(jnp.bfloat16)
    key_grad = (
        jnp.sum(key_parts.astype(jnp.float32), axis=0)
        .astype(jnp.bfloat16)
        .reshape(row_count, col_count)
    )
    value_grad = (
        jnp.sum(value_parts.astype(jnp.float32), axis=0)
        .astype(jnp.bfloat16)
        .reshape(row_count, col_count)
    )
    query_terms = score_scale * jnp.einsum(
        "hqk,khd->qhd", score_grad, key_heads, preferred_element_type=jnp.float32
    )
    query_sum = lax.psum(
        query_terms.reshape(dec_tokens, col_count).astype(jnp.bfloat16), "seq"
    ).astype(jnp.float32)
    query_grad = lax.dynamic_slice_in_dim(query_sum, dec_offset, row_count, 0).astype(jnp.bfloat16)
    contract = (((1,), (1,)), ((), ()))
    grad_terms = lax.dot_general(
        key_grad, kv_weight[0], contract, preferred_element_type=jnp.float32
    ) + lax.dot_general(value_grad, kv_weight[1], contract, preferred_element_type=jnp.float32)
    final_term = jnp.where(is_enc, grad_terms, out_part)
    final_share = lax.psum_scatter(
        final_term.astype(jnp.bfloat16), "mp", scatter_dimension=1, tiled=True
    ).astype(jnp.float32)
    base_rows = jnp.where(is_enc, cotangent, residual).astype(jnp.float32)
    final_rows = (base_rows + final_share).astype(jnp.bfloat16)
    states_out = jnp.where(is_enc, encoder_out, final_rows)
    grad_states = jnp.where(is_enc, final_rows, query_grad)
    return (states_out, grad_states)


def solution(mesh):
    return jax.shard_map(
        shards,
        mesh=mesh,
        in_specs=(
            P("seq", "mp"),
            P(None, "seq", "mp"),
            P("seq", "mp"),
            P("seq", "mp"),
            P(None, "mp", None),
            P(None, None, "mp"),
            P(),
            P("mp"),
        ),
        out_specs=(P("seq", "mp"), P("seq", "mp")),
        check_vma=False,
    )
```

profile of v0, /device:TPU:2, one launch (start us, length us, event | category | flops | bytes accessed | tf_op | source)
XLA Modules:
  0.0 338.7 jit_solution(7236549203202645054)
XLA Ops:
  8.0 0.0 all-gather.7.cloned.1.call-start
  8.1 0.7 all-gather.7.cloned.1.call-update
  8.8 0.0 all-reduce.4.cloned.1.call-start
  8.8 1.2 copy.30
  10.1 0.1 fusion.57
  10.2 1.9 collective-permute-start
  12.1 3.6 %collective-permute-start.1 = (bf16[2,127,512]{1,2,0:T(8,128)(2,1)S(1)}, bf16[2,127,512]{1,2,0:T(8,128)(2,1)S(1)}, u32[]{:S(2)}, u32[]{:S(2)}) collective-permute-start(bf16[2,127,512]{1,2,0:T(8,128)(2,1)S(1)} %get-tuple-element.187), channel_id=1, source_target_pairs={{8,0},{16,8},{24,16},{9,1},{17,9},{25,17},{10,2},{18,10},{26,18},{... | collective-permute-start | bytes 780296 | tf_op jit(solution)/shard_map/ppermute | solution.py:20
  15.8 2.1 collective-permute-done
  17.9 2.3 collective-permute-done.1
  20.2 0.5 pad_maximum_fusion
  20.8 8.5 %conditional.4 = (bf16[256,4096]{1,0:T(8,128)(2,1)S(1)}) conditional(s32[]{:T(128)} %convert_element_type.116, () %tuple.47, (s32[]{:T(128)}, s32[2,1024]{1,0:T(2,128)S(1)}, s32[]{:T(128)}, s32[256]{0:T(256)S(1)}, s32[8]{0:T(128)S(1)}, /*index=5*/bf16[256,512]{1,0:T(8,128)(2,1)S(1)}, bf16[2,510,512]{1,2,0:T(8,128)(2,1)S(1)}, ...), branch_computations={%region_0.0_spmd, %region_1.4_spmd} | conditional | flops 1489188096 | bytes 13526646 | solution.py:81
  20.8 0.1 constant_dynamic-slice_fusion
  20.9 0.2 compare_and_fusion
  21.1 0.1 copy.33
  21.2 0.1 subtract_abs_fusion
  21.4 0.1 fusion.54
  21.5 2.0 fusion.56
  23.5 2.3 fusion.11
  25.8 3.5 %fusion.1 = bf16[256,4096]{1,0:T(8,128)(2,1)S(1)} fusion(bf16[256,512]{0,1:T(8,128)(2,1)S(1)} %bitcast.107, bf16[2,512,4096]{2,1,0:T(8,128)(2,1)} %get-tuple-element.145), kind=kOutput, calls=%fused_computation.1 | convolution fusion | flops 1073741824 | bytes 6553600 | tf_op jit(solution)/shard_map/cond/branch_1_fun/dot_general | solution.py:77
  29.3 1.3 copy-done.2
  30.6 0.0 all-gather.5.cloned.1.call-start
  30.7 0.7 all-gather.5.cloned.1.call-update
  31.4 0.0 all-gather.9.cloned.1.call-start
  31.4 0.7 all-gather.9.cloned.1.call-update
  32.1 0.0 all-reduce.6.cloned.1.call-start
  32.2 0.1 compare_and_fusion.1
  32.4 1.0 slice.90
  33.3 0.1 copy.34
  33.5 132.4 %all-reduce.4.cloned.1.call-done = bf16[256,4096]{1,0:T(8,128)(2,1)} async-done(((bf16[256,4096]{1,0:T(8,128)(2,1)}), bf16[256,4096]{1,0:T(8,128)(2,1)}) %all-reduce.4.cloned.1.call-update) | async-done | bytes 2097168 | tf_op jit(solution)/shard_map/psum | solution.py:84
  165.9 4.3 %add_convert_fusion = bf16[256,4096]{1,0:T(8,128)(2,1)} fusion(bf16[256,4096]{1,0:T(8,128)(2,1)} %all-reduce.4.cloned.1.call-done, bf16[256,4096]{1,0:T(8,128)(2,1)} %all-gather.5.cloned.1.call-done), kind=kLoop, calls=%fused_computation.49 | loop fusion | flops 4194304 | bytes 6291456 | tf_op jit(solution)/shard_map/convert_element_type | solution.py:85
  170.3 8.3 %conditional.5 = (bf16[256,8,64]{0,2,1:T(8,128)(2,1)S(1)}, bf16[256,8,64]{0,2,1:T(8,128)(2,1)S(1)}) conditional(s32[]{:T(128)} %convert_element_type.116, () %tuple.49, (bf16[2,4096,512]{2,1,0:T(8,128)(2,1)}, bf16[256,4096]{1,0:T(8,128)(2,1)}) %tuple.50), branch_computations={%region_5.6_spmd, %region_6.7_spmd} | conditional | flops 2147745792 | bytes 47710252 | solution.py:99
  170.3 4.2 %fusion.29 = bf16[256,512]{1,0:T(8,128)(2,1)S(1)} fusion(bf16[256,4096]{1,0:T(8,128)(2,1)} %get-tuple-element.146, bf16[2,4096,512]{2,1,0:T(8,128)(2,1)} %get-tuple-element.147), kind=kOutput, calls=%fused_computation.33 | convolution fusion | flops 1073872896 | bytes 6553600 | tf_op jit(solution)/shard_map/cond/branch_1_fun/dot_general | solution.py:94
  174.5 1.0 copy-done.1
  175.5 2.8 fusion.26
  178.3 0.1 copy.28
  178.5 0.1 copy.29
  178.6 0.5 fusion.59
  179.1 6.1 %pmax.7 = f32[8,256]{1,0:T(8,128)S(1)} all-reduce(f32[8,256]{1,0:T(8,128)S(1)} %get-tuple-element.190), channel_id=1, replica_groups=mesh['seq'=4,'mp'=8] {'seq'}, use_global_device_ids=true, to_apply=%region_8.9 | all-reduce | flops 2048 | bytes 16384 | tf_op jit(solution)/shard_map/pmax | solution.py:120
  185.2 0.3 fusion.49
  185.6 5.9 %psum.29 = f32[8,256]{1,0:T(8,128)S(1)} all-reduce(f32[8,256]{1,0:T(8,128)S(1)} %fusion.49), channel_id=1, replica_groups=mesh['seq'=4,'mp'=8] {'seq'}, use_global_device_ids=true, to_apply=%region_10.11 | all-reduce | flops 2048 | bytes 16384 | tf_op jit(solution)/shard_map/psum | solution.py:122
  191.4 0.3 fusion.52
  191.8 1.0 convolution_convert_fusion.1
  192.8 0.0 all-gather.11.cloned.1.call-start
  192.9 0.2 conditional.6
  193.1 0.7 copy-done.12
  193.8 0.0 all-reduce.8.cloned.1.call-start
  193.9 29.0 %all-reduce.6.cloned.1.call-done = bf16[256,512]{0,1:T(8,128)(2,1)} async-done(((bf16[256,512]{0,1:T(8,128)(2,1)}), bf16[256,512]{0,1:T(8,128)(2,1)}) %all-reduce.6.cloned.1.call-update) | async-done | bytes 262160 | tf_op jit(solution)/shard_map/psum | solution.py:128
  222.9 1.5 conditional.7
  222.9 1.5 broadcast.157
  224.4 17.5 %all-gather.11.cloned.1.call-done = bf16[1024,512]{1,0:T(8,128)(2,1)} async-done(((bf16[256,512]{1,0:T(8,128)(2,1)}), bf16[1024,512]{1,0:T(8,128)(2,1)}) %all-gather.11.cloned.1.call-update) | async-done | bytes 1048592 | tf_op jit(solution)/shard_map/all_gather | solution.py:139
  241.9 1.7 slice.91
  243.6 1.1 copy.35
  244.7 1.1 convolution_convert_fusion
  245.8 1.0 fusion.53
  246.9 1.7 multiply_convert_fusion
  248.5 0.3 fusion.51
  248.9 0.4 fusion.50
  249.3 0.8 copy.42
  250.2 0.0 reduce-scatter.2.cloned.1.call-start
  250.2 3.6 %fusion.44 = f32[256,4096]{1,0:T(8,128)S(1)} fusion(bf16[256,512]{0,1:T(8,128)(2,1)S(1)} %bitcast.100, bf16[2,4096,512]{2,1,0:T(8,128)(2,1)} %param.21), kind=kOutput, calls=%fused_computation.45 | convolution fusion | flops 1073741824 | bytes 8650752 | tf_op jit(solution)/shard_map/dot_general | solution.py:182
  253.9 5.0 %fusion.42 = bf16[256,4096]{1,0:T(8,128)(2,1)} fusion(bf16[256,4096]{1,0:T(8,128)(2,1)S(1)} %copy-done, f32[256,4096]{1,0:T(8,128)S(1)} %fusion.44, bf16[256,512]{0,1:T(8,128)(2,1)S(1)} %bitcast.99, bf16[2,4096,512]{2,1,0:T(8,128)(2,1)} %param.21, pred[]{:T(512)S(6)} %lt.14), kind=kOutput, calls=%fused_computation.43 | convolution fusion | flops 1075838976 | bytes 12845057 | tf_op jit(solution)/shard_map/dot_general | solution.py:184
  259.0 23.4 %all-reduce.8.cloned.1.call-done = bf16[256,512]{1,0:T(8,128)(2,1)} async-done(((bf16[256,512]{1,0:T(8,128)(2,1)}), bf16[256,512]{1,0:T(8,128)(2,1)}) %all-reduce.8.cloned.1.call-update) | async-done | bytes 262160 | tf_op jit(solution)/shard_map/psum | solution.py:177
  282.4 46.9 %reduce-scatter.2.cloned.1.call-done = bf16[256,512]{1,0:T(8,128)(2,1)} async-done(((bf16[256,4096]{1,0:T(8,128)(2,1)}), bf16[256,512]{1,0:T(8,128)(2,1)}) %reduce-scatter.2.cloned.1.call-update) | async-done | bytes 262160 | tf_op jit(solution)/shard_map/reduce_scatter | solution.py:186
  329.3 2.0 broadcast_select_fusion
  (42 shorter events, 0.2 us)
Async XLA Ops:
  8.0 12.7 %copy-start.9 = (bf16[256,512]{1,0:T(8,128)(2,1)S(1)}, bf16[256,512]{1,0:T(8,128)(2,1)}, u32[]{:S(2)}) copy-start(bf16[256,512]{1,0:T(8,128)(2,1)} %param.16) | copy-start | bytes 786436
  8.0 12.7 %copy-start.13 = (s32[2,1024]{1,0:T(2,128)S(1)}, s32[2,1024]{1,0:T(2,128)}, u32[]{:S(2)}) copy-start(s32[2,1024]{1,0:T(2,128)} %param.22) | copy-start | bytes 24580
  8.0 12.7 %copy-start.14 = (s32[8]{0:T(128)S(1)}, s32[8]{0:T(128)}, u32[]{:S(2)}) copy-start(s32[8]{0:T(128)} %param.23) | copy-start | bytes 100
  8.0 24.3 %all-gather.7.cloned.1.call-start = ((), (), s32[]{:S(2)}) async-start(), calls=%async_computation.3 | async-start | bytes 1310720 | tf_op jit(solution)/shard_map/all_gather | solution.py:108
  8.8 157.1 %all-reduce.4.cloned.1.call-start = ((), (), s32[]{:S(2)}) async-start(), calls=%async_computation.2 | async-start | bytes 4194304 | tf_op jit(solution)/shard_map/psum | solution.py:84
  10.2 7.7 %collective-permute-start = (bf16[2,127,512]{1,2,0:T(8,128)(2,1)S(1)}, bf16[2,127,512]{1,2,0:T(8,128)(2,1)S(1)}, u32[]{:S(2)}, u32[]{:S(2)}) collective-permute-start(bf16[2,127,512]{1,2,0:T(8,128)(2,1)S(1)} %get-tuple-element.186), channel_id=1, source_target_pairs={{0,8},{8,16},{16,24},{1,9},{9,17},{17,25},{2,10},{10,18},{18,26},{... | collective-permute-start | bytes 780296 | tf_op jit(solution)/shard_map/ppermute | solution.py:18
  12.1 8.1 %collective-permute-start.1 = (bf16[2,127,512]{1,2,0:T(8,128)(2,1)S(1)}, bf16[2,127,512]{1,2,0:T(8,128)(2,1)S(1)}, u32[]{:S(2)}, u32[]{:S(2)}) collective-permute-start(bf16[2,127,512]{1,2,0:T(8,128)(2,1)S(1)} %get-tuple-element.187), channel_id=1, source_target_pairs={{8,0},{16,8},{24,16},{9,1},{17,9},{25,17},{10,2},{18,10},{26,18},{... | collective-permute-start | bytes 780296 | tf_op jit(solution)/shard_map/ppermute | solution.py:20
  29.3 1.3 copy-start.2
  30.6 135.3 %all-gather.5.cloned.1.call-start = ((), (), s32[]{:S(2)}) async-start(), calls=%async_computation.1 | async-start | bytes 2359296 | tf_op jit(solution)/shard_map/all_gather | solution.py:53
  31.4 161.5 %all-gather.9.cloned.1.call-start = ((), (), s32[]{:S(2)}) async-start(), calls=%async_computation.4 | async-start | bytes 2359296 | tf_op jit(solution)/shard_map/all_gather | solution.py:54
  32.1 190.7 %all-reduce.6.cloned.1.call-start = ((), (), s32[]{:S(2)}) async-start(), calls=%async_computation.6 | async-start | bytes 524288 | tf_op jit(solution)/shard_map/psum | solution.py:128
  33.5 145.2 %copy-start.3 = (bf16[256,512]{0,1:T(8,128)(2,1)}, bf16[256,512]{0,1:T(8,128)(2,1)S(1)}, u32[]{:S(2)}) copy-start(bf16[256,512]{0,1:T(8,128)(2,1)S(1)} %copy.34) | copy-start | bytes 786436
  170.3 5.2 %copy-start.1 = (bf16[2,4096,512]{2,1,0:T(8,128)(2,1)S(1)}, bf16[2,4096,512]{2,1,0:T(8,128)(2,1)}, u32[]{:S(2)}) copy-start(bf16[2,4096,512]{2,1,0:T(8,128)(2,1)} %get-tuple-element.147) | copy-start | bytes 25165828 | tf_op jit(solution)/shard_map/cond
  178.6 7.0 %copy-start.5 = (bf16[256,8,64]{0,2,1:T(8,128)(2,1)}, bf16[256,8,64]{0,2,1:T(8,128)(2,1)S(1)}, u32[]{:S(2)}) copy-start(bf16[256,8,64]{0,2,1:T(8,128)(2,1)S(1)} %get-tuple-element.156) | copy-start | bytes 786436
  178.6 14.2 %copy-start.11 = (bf16[256,8,64]{0,2,1:T(8,128)(2,1)}, bf16[256,8,64]{0,2,1:T(8,128)(2,1)S(1)}, u32[]{:S(2)}) copy-start(bf16[256,8,64]{0,2,1:T(8,128)(2,1)S(1)} %get-tuple-element.157) | copy-start | bytes 786436
  192.8 49.1 %all-gather.11.cloned.1.call-start = ((), (), s32[]{:S(2)}) async-start(), calls=%async_computation.5 | async-start | bytes 1310720 | tf_op jit(solution)/shard_map/all_gather | solution.py:139
  193.1 0.7 copy-start.12
  193.8 88.5 %all-reduce.8.cloned.1.call-start = ((), (), s32[]{:S(2)}) async-start(), calls=%async_computation.8 | async-start | bytes 524288 | tf_op jit(solution)/shard_map/psum | solution.py:177
  246.8 1.7 copy-start.6
  246.8 2.0 copy-start.4
  250.2 79.1 %reduce-scatter.2.cloned.1.call-start = ((), (), s32[]{:S(2)}) async-start(), calls=%async_computation.7 | async-start | bytes 2359296 | tf_op jit(solution)/shard_map/reduce_scatter | solution.py:186
  250.2 3.7 %copy-start = (bf16[256,4096]{1,0:T(8,128)(2,1)S(1)}, bf16[256,4096]{1,0:T(8,128)(2,1)}, u32[]{:S(2)}) copy-start(bf16[256,4096]{1,0:T(8,128)(2,1)} %get-tuple-element.198) | copy-start | bytes 6291460
  250.2 3.7 %copy-start.10 = (bf16[8,64,256]{2,1,0:T(8,128)(2,1)S(1)}, bf16[8,64,256]{2,1,0:T(8,128)(2,1)}, u32[]{:S(2)}) copy-start(bf16[8,64,256]{2,1,0:T(8,128)(2,1)} %convolution_convert_fusion) | copy-start | bytes 786436
  253.9 75.4 %copy-start.7 = (bf16[256,512]{1,0:T(8,128)(2,1)S(1)}, bf16[256,512]{1,0:T(8,128)(2,1)}, u32[]{:S(2)}) copy-start(bf16[256,512]{1,0:T(8,128)(2,1)} %param.18) | copy-start | bytes 786436
  253.9 75.4 %copy-start.8 = (bf16[256,512]{1,0:T(8,128)(2,1)S(1)}, bf16[256,512]{1,0:T(8,128)(2,1)}, u32[]{:S(2)}) copy-start(bf16[256,512]{1,0:T(8,128)(2,1)} %param.19) | copy-start | bytes 786436
Sparse Core Ops, SparseCore 0:
  10.4 16.7 all-gather.6
  33.5 68.8 all-gather.4
  104.4 66.6 all-gather.8
  192.9 29.9 all-reduce.5
  224.9 16.9 all-gather.10
  250.3 32.0 all-reduce.7
Sparse Core Ops, SparseCore 1:
  30.7 135.1 all-reduce.3
  259.0 70.2 reduce-scatter.1
where the time goes:
time: 341 us; the launch traced here: 339 us
  waiting for transfers between devices  256 us (75%)
  matrix products  28.6 us (8%)
  between operations  15.9 us (5%)
  blocking collectives  12 us (4%)
  local copies, waits for them, and re-layouts  11.3 us (3%)
  other arithmetic  8.97 us (3%)
  starting transfers between devices  5.89 us (2%)
    psum x1, waiting for transfers between devices, shards(): lax.psum(head_partial.astype(jnp.bfloat16), 'mp').astype(jnp.float32)  132 us
    reduce_scatter x1, waiting for transfers between devices, shards(): lax.psum_scatter(final_term.astype(jnp.bfloat16), 'mp', scatter_dimension...  46.9 us
    psum x1, waiting for transfers between devices, shards(): context_all = lax.psum(partial_ctx.astype(jnp.bfloat16), 'seq')  29 us
    psum x1, waiting for transfers between devices, shards(): lax.psum(query_terms.reshape(dec_tokens, col_count).astype(jnp.bfloat16),...  23.4 us
    all_gather x1, waiting for transfers between devices, shards(): grad_all = lax.all_gather(grad_own, 'seq', axis=0, tiled=True)[enc_tokens:]  17.5 us
  transfers between devices with their start and end apart: 10, of which 7 were waited for; matrix products, arithmetic and copies ran while one was open for 10% of the time, Pallas kernels for 0%

commit v1 on v0

--- a/solution.py
+++ b/solution.py
@@ -1,6 +1,10 @@
+import functools
+
 import jax
 import jax.numpy as jnp
 from jax import lax
+from jax.experimental import pallas as pl
+from jax.experimental.pallas import tpu as pltpu
 from jax.sharding import PartitionSpec as P
 
 HD = 64
@@ -193,9 +197,604 @@
     return (states_out, grad_states)
 
 
+F32 = jnp.float32
+BF16 = jnp.bfloat16
+LOW = -1e30
+PAIR = 2 * HD
+HALO = 128
+NT = (((1,), (1,)), ((), ()))
+
+
+def dot(a, b):
+    return jnp.dot(a, b, preferred_element_type=F32)
+
+
+def dot_nt(a, b):
+    return lax.dot_general(a, b, NT, preferred_element_type=F32)
+
+
+def layer_kernel(
+    slabs,
+    groups,
+    q_ref,
+    kv_ref,
+    res_ref,
+    cot_ref,
+    ow_ref,
+    kw_ref,
+    bnd_ref,
+    win_ref,
+    states_ref,
+    grads_ref,
+    w_out,
+    w_kv,
+    kv_all,
+    ctx,
+    own_part,
+    ysend,
+    yrecv,
+    zsend,
+    zrecv,
+    ysend2,
+    yrecv2,
+    zsend2,
+    zrecv2,
+    gath,
+    acc,
+    kv_new,
+    dq,
+    dg,
+    e_buf,
+    d_buf,
+    stat,
+    stat_in,
+    fac,
+    tbuf,
+    ctx_in,
+    qg_buf,
+    qg_in,
+    kvg,
+    w_sem,
+    kv_sem,
+    halo_s,
+    halo_r,
+    ys_s,
+    yr_s,
+    zs_s,
+    zr_s,
+    ys2_s,
+    yr2_s,
+    zs2_s,
+    zr2_s,
+    gz_s,
+    gz_r,
+    gy_s,
+    gy_r,
+    dq_s,
+    dq_r,
+    dg_s,
+    dg_r,
+    st_s,
+    st_r,
+    cx_s,
+    cx_r,
+    qg_s,
+    qg_r,
+):
+    rows, cols = q_ref.shape
+    pairs = cols // PAIR
+    heads = cols // HD
+    enc = slabs - 1
+    nz = groups // 2
+    scale = HD ** (-0.5)
+    s = lax.axis_index("seq")
+    g = lax.axis_index("mp")
+    z = g // 2
+    y = lax.rem(g, 2)
+    yo = 1 - y
+
+    def remote(src, dst, send, recv, seq, mp):
+        return pltpu.make_async_remote_copy(
+            src_ref=src,
+            dst_ref=dst,
+            send_sem=send,
+            recv_sem=recv,
+            device_id={"seq": seq, "mp": mp},
+            device_id_type=pl.DeviceIdType.MESH,
+        )
+
+    def arrived(dst, recv):
+        pltpu.make_async_copy(dst, dst, recv).wait()
+
+    is_enc = s < enc
+    is_dec = s >= enc
+
+    @pl.when(is_enc)
+    def _():
+        pltpu.make_async_copy(kv_ref, kv_all.at[:, pl.ds(HALO, rows)], kv_sem).start()
+        pltpu.make_async_copy(ow_ref.at[0], w_out, w_sem.at[0]).start()
+        pltpu.make_async_copy(kw_ref, w_kv, w_sem.at[1]).start()
+
+    @pl.when(is_dec)
+    def _():
+        pltpu.make_async_copy(ow_ref.at[1], w_out, w_sem.at[0]).start()
+
+    barrier = pltpu.get_barrier_semaphore()
+    for k in range(1, slabs):
+        pl.semaphore_signal(
+            barrier,
+            inc=1,
+            device_id={"seq": lax.rem(s + k, slabs), "mp": g},
+            device_id_type=pl.DeviceIdType.MESH,
+        )
+    for k in range(1, nz):
+        pl.semaphore_signal(
+            barrier,
+            inc=1,
+            device_id={"seq": s, "mp": lax.rem(z + k, nz) * 2 + y},
+            device_id_type=pl.DeviceIdType.MESH,
+        )
+    pl.semaphore_signal(
+        barrier,
+        inc=1,
+        device_id={"seq": s, "mp": z * 2 + yo},
+        device_id_type=pl.DeviceIdType.MESH,
+    )
+    pl.semaphore_wait(barrier, slabs - 1 + nz - 1 + 1)
+
+    lane = lax.broadcasted_iota(jnp.int32, (1, PAIR), 1)
+    low_lane = lane < HD
+    lane_masks = (
+        jnp.where(low_lane, 1.0, 0.0).astype(BF16),
+        jnp.where(low_lane, 0.0, 1.0).astype(BF16),
+    )
+    low_row = lax.broadcasted_iota(jnp.int32, (PAIR, 1), 0) < HD
+
+    def pair_cols(p):
+        return pl.ds(pl.multiple_of(p * PAIR, PAIR), PAIR)
+
+    def chunk_cols(c):
+        return pl.ds(pl.multiple_of(c * cols, cols), cols)
+
+    def reduce_scatter(part, ysend, yrecv, zsend, zrecv, ys, yr, zs, zr):
+        def first(k, carry):
+            zt = lax.rem(z + 2 + k, nz)
+            ysend[zt] = part(zt * 2 + yo)
+            remote(ysend.at[zt], yrecv.at[zt], ys.at[zt], yr.at[zt], s, z * 2 + yo).start()
+            return carry
+
+        lax.fori_loop(0, nz, first, 0)
+
+        def own(k, carry):
+            zt = lax.rem(z + 2 + k, nz)
+            own_part[zt] = part(zt * 2 + y)
+            return carry
+
+        lax.fori_loop(0, nz, own, 0)
+
+        def second(k, carry):
+            zt = lax.rem(z + 2 + k, nz)
+            arrived(yrecv.at[zt], yr.at[zt])
+            both = own_part[zt].astype(F32) + yrecv[zt].astype(F32)
+
+            @pl.when(zt != z)
+            def _():
+                zsend[zt] = both.astype(BF16)
+                remote(zsend.at[zt], zrecv.at[z], zs.at[zt], zr.at[z], s, zt * 2 + y).start()
+
+            @pl.when(zt == z)
+            def _():
+                acc[0] = both
+
+            return carry
+
+        lax.fori_loop(0, nz, second, 0)
+
+        def third(k, carry):
+            zt = lax.rem(z + k, nz)
+            arrived(zrecv.at[zt], zr.at[zt])
+            acc[0] = acc[0] + zrecv[zt].astype(F32)
+            return carry
+
+        lax.fori_loop(1, nz, third, 0)
+        return acc[0]
+
+    def end_scatter(ysend, zsend, ys, zs):
+        def last(k, carry):
+            arrived(ysend.at[k], ys.at[k])
+            return carry
+
+        lax.fori_loop(0, nz, last, 0)
+
+        def last_z(k, carry):
+            zt = lax.rem(z + k, nz)
+            arrived(zsend.at[zt], zs.at[zt])
+            return carry
+
+        lax.fori_loop(1, nz, last_z, 0)
+
+    def gather(use):
+        remote(gath.at[g], gath.at[g], gy_s.at[z], gy_r.at[z], s, z * 2 + yo).start()
+
+        def spread(k, carry):
+            zt = lax.rem(z + 1 + k, nz)
+            remote(gath.at[g], gath.at[g], gz_s.at[zt], gz_r.at[z], s, zt * 2 + y).start()
+            return carry
+
+        lax.fori_loop(0, nz - 1, spread, 0)
+
+        def begin(k, carry):
+            zt = lax.rem(z + k, nz)
+            c = zt * 2 + y
+
+            @pl.when(k > 0)
+            def _():
+                arrived(gath.at[c], gz_r.at[zt])
+                remote(gath.at[c], gath.at[c], gy_s.at[zt], gy_r.at[zt], s, z * 2 + yo).start()
+
+            use(c)
+            return carry
+
+        lax.fori_loop(0, nz, begin, 0)
+
+        def finish(k, carry):
+            zt = lax.rem(z + k, nz)
+            c = zt * 2 + yo
+            arrived(gath.at[c], gy_r.at[zt])
+            use(c)
+            return carry
+
+        lax.fori_loop(0, nz, finish, 0)
+
+    def end_gather():
+        def last(k, carry):
+            arrived(gath.at[k * 2 + y], gy_s.at[k])
+            return carry
+
+        lax.fori_loop(0, nz, last, 0)
+
+        def last_z(k, carry):
+            zt = lax.rem(z + k, nz)
+            arrived(gath.at[g], gz_s.at[zt])
+            return carry
+
+        lax.fori_loop(1, nz, last_z, 0)
+
+    def joint_stats():
+        top = stat_in[0, 0]
+        for i in range(1, enc):
+            top = jnp.maximum(top, stat_in[i, 0])
+        total = jnp.zeros_like(top)
+        dots = jnp.zeros_like(top)
+        for i in range(enc):
+            shift = jnp.exp(stat_in[i, 0] - top)
+            total = total + shift * stat_in[i, 1]
+            dots = dots + shift * stat_in[i, 2]
+        return top, total, dots
+
+    @pl.when(is_enc)
+    def _():
+        @pl.when(s + 1 < enc)
+        def _():
+            remote(
+                kv_ref.at[:, pl.ds(rows - HALO, HALO)],
+                kv_all.at[:, pl.ds(0, HALO)],
+                halo_s.at[0],
+                halo_r.at[0],
+                s + 1,
+                g,
+            ).start()
+
+        @pl.when(s > 0)
+        def _():
+            remote(
+                kv_ref.at[:, pl.ds(0, HALO)],
+                kv_all.at[:, pl.ds(HALO + rows, HALO)],
+                halo_s.at[1],
+                halo_r.at[1],
+                s - 1,
+                g,
+            ).start()
+
+        @pl.when(s == 0)
+        def _():
+            kv_all[:, pl.ds(0, HALO)] = jnp.zeros((2, HALO, cols), BF16)
+
+        @pl.when(s == enc - 1)
+        def _():
+            kv_all[:, pl.ds(HALO + rows, HALO)] = jnp.zeros((2, HALO, cols), BF16)
+
+        pltpu.make_async_copy(kv_ref, kv_all.at[:, pl.ds(HALO, rows)], kv_sem).wait()
+
+        @pl.when(s > 0)
+        def _():
+            arrived(kv_all.at[:, pl.ds(0, HALO)], halo_r.at[0])
+
+        @pl.when(s + 1 < enc)
+        def _():
+            arrived(kv_all.at[:, pl.ds(HALO + rows, HALO)], halo_r.at[1])
+
+        span = rows + 2 * HALO
+        key_pos = s * rows - HALO + lax.broadcasted_iota(jnp.int32, (span, 1), 0)
+        own_pos = s * rows + lax.broadcasted_iota(jnp.int32, (1, rows), 1)
+        far = jnp.abs(key_pos - own_pos)
+        in_doc = (key_pos >= bnd_ref[0:1, :]) & (key_pos <= bnd_ref[1:2, :])
+        far = jnp.where(in_doc, far, jnp.int32(1 << 20))
+
+        def local_pair(p, carry):
+            at = pair_cols(p)
+            q_pair = q_ref[:, at]
+            k_pair = kv_all[0, :, at]
+            v_t = kv_all[1, :, at].T
+            got = []
+            for i in range(2):
+                sc = dot_nt(k_pair, q_pair * lane_masks[i]) * scale
+                sc = jnp.where(far <= win_ref[p * 2 + i], sc, LOW)
+                e = jnp.exp(sc - jnp.max(sc, axis=0, keepdims=True))
+                inv = 1.0 / jnp.sum(e, axis=0, keepdims=True)
+                got.append(dot(v_t, (e * inv).astype(BF16)))
+            ctx[:, at] = jnp.where(low_row, got[0], got[1]).T.astype(BF16)
+            return carry
+
+        lax.fori_loop(0, pairs, local_pair, 0)
+        pltpu.make_async_copy(ow_ref.at[0], w_out, w_sem.at[0]).wait()
+        total = reduce_scatter(
+            lambda c: dot(ctx[...], w_out[:, chunk_cols(c)]).astype(BF16),
+            ysend,
+            yrecv,
+            zsend,
+            zrecv,
+            ys_s,
+            yr_s,
+            zs_s,
+            zr_s,
+        )
+        hidden = (res_ref[...].astype(F32) + total).astype(BF16)
+        gath[g] = hidden
+        states_ref[...] = hidden
+        acc[...] = jnp.zeros_like(acc)
+        pltpu.make_async_copy(kw_ref, w_kv, w_sem.at[1]).wait()
+
+        def project(c):
+            block = gath[c]
+            acc[0] = acc[0] + dot(block, w_kv[0, chunk_cols(c), :])
+            acc[1] = acc[1] + dot(block, w_kv[1, chunk_cols(c), :])
+
+        gather(project)
+        kv_new[...] = acc[...].astype(BF16)
+        arrived(dq, dq_r)
+        arrived(dg, dg_r)
+
+        tok_pos = s * rows + lax.broadcasted_iota(jnp.int32, (rows, 1), 0)
+        seen = (tok_pos >= bnd_ref[2:3, :]) & (tok_pos <= bnd_ref[3:4, :])
+
+        def cross_pair(p, carry):
+            at = pair_cols(p)
+            q_pair = dq[:, at]
+            g_pair = dg[:, at]
+            k_pair = kv_new[0, :, at]
+            v_pair = kv_new[1, :, at]
+            v_t = v_pair.T
+            got = []
+            for i in range(2):
+                sc = dot_nt(k_pair, q_pair * lane_masks[i]) * scale
+                sc = jnp.where(seen, sc, LOW)
+                top = jnp.max(sc, axis=0, keepdims=True)
+                e = jnp.exp(sc - top)
+                dp = dot_nt(v_pair, g_pair * lane_masks[i])
+                h = p * 2 + i
+                e_buf[h] = e
+                d_buf[h] = dp
+                stat[0, pl.ds(h, 1), :] = top
+                stat[1, pl.ds(h, 1), :] = jnp.sum(e, axis=0, keepdims=True)
+                stat[2, pl.ds(h, 1), :] = jnp.sum(e * dp, axis=0, keepdims=True)
+                got.append(dot(v_t, e.astype(BF16)))
+            tbuf[pair_cols(p), :] = jnp.where(low_row, got[0], got[1]).astype(BF16)
+            return carry
+
+        lax.fori_loop(0, pairs, cross_pair, 0)
+        for k in range(1, slabs):
+            to = lax.rem(s + k, slabs)
+            remote(stat, stat_in.at[s], st_s.at[k - 1], st_r.at[s], to, g).start()
+        remote(tbuf, ctx_in.at[s], cx_s, cx_r.at[s], enc, g).start()
+        stat_in[s] = stat[...]
+        for k in range(1, enc):
+            at = lax.rem(s + k, enc)
+            arrived(stat_in.at[at], st_r.at[at])
+        top, total, dots = joint_stats()
+        fac[0] = jnp.exp(stat[0] - top) / total
+        fac[1] = dots / total
+
+        def grad_pair(p, carry):
+            at = pair_cols(p)
+            q_pair = dq[:, at]
+            g_pair = dg[:, at]
+            k_t = kv_new[0, :, at].T
+            kg, vg, qg = [], [], []
+            for i in range(2):
+                h = p * 2 + i
+                w = e_buf[h] * fac[0, pl.ds(h, 1), :]
+                ds = (w * (d_buf[h] - fac[1, pl.ds(h, 1), :])).astype(BF16)
+                vg.append(dot(w.astype(BF16), g_pair))
+                kg.append(dot(ds, q_pair))
+                qg.append(dot(k_t, ds))
+            kvg[0, :, at] = (scale * jnp.where(low_lane, kg[0], kg[1])).astype(BF16)
+            kvg[1, :, at] = jnp.where(low_lane, vg[0], vg[1]).astype(BF16)
+            qg_buf[pair_cols(p), :] = (scale * jnp.where(low_row, qg[0], qg[1])).astype(BF16)
+            return carry
+
+        lax.fori_loop(0, pairs, grad_pair, 0)
+        remote(qg_buf, qg_in.at[s], qg_s, qg_r.at[s], enc, g).start()
+        total = reduce_scatter(
+            lambda c: (
+                dot_nt(kvg[0], w_kv[0, chunk_cols(c), :]) + dot_nt(kvg[1], w_kv[1, chunk_cols(c), :])
+            ).astype(BF16),
+            ysend2,
+            yrecv2,
+            zsend2,
+            zrecv2,
+            ys2_s,
+            yr2_s,
+            zs2_s,
+            zr2_s,
+        )
+        grads_ref[...] = (cot_ref[...].astype(F32) + total).astype(BF16)
+
+        @pl.when(s + 1 < enc)
+        def _():
+            arrived(kv_ref.at[:, pl.ds(rows - HALO, HALO)], halo_s.at[0])
+
+        @pl.when(s > 0)
+        def _():
+            arrived(kv_ref.at[:, pl.ds(0, HALO)], halo_s.at[1])
+
+        end_scatter(ysend, zsend, ys_s, zs_s)
+        end_gather()
+        for k in range(1, slabs):
+            arrived(stat, st_s.at[k - 1])
+        arrived(tbuf, cx_s)
+        arrived(qg_buf, qg_s)
+        end_scatter(ysend2, zsend2, ys2_s, zs2_s)
+
+    @pl.when(is_dec)
+    def _():
+        for k in range(enc):
+            remote(q_ref, dq, dq_s.at[k], dq_r, k, g).start()
+        gath[g] = cot_ref[...]
+        acc[0] = jnp.zeros((rows, cols), F32)
+        pltpu.make_async_copy(ow_ref.at[1], w_out, w_sem.at[0]).wait()
+
+        def back(c):
+            acc[0] = acc[0] + dot_nt(gath[c], w_out[:, chunk_cols(c)])
+
+        gather(back)
+        dg[...] = acc[0].astype(BF16)
+        for k in range(enc):
+            remote(dg, dg, dg_s.at[k], dg_r, k, g).start()
+        for k in range(enc):
+            arrived(stat_in.at[k], st_r.at[k])
+        top, total, dots = joint_stats()
+        shares = [jnp.exp(stat_in[k, 0] - top) / total for k in range(enc)]
+        for k in range(enc):
+            arrived(ctx_in.at[k], cx_r.at[k])
+        for h in range(heads):
+            at = slice(h * HD, (h + 1) * HD)
+            part = jnp.zeros((HD, rows), F32)
+            for k in range(enc):
+                part = part + shares[k][h : h + 1, :] * ctx_in[k, at, :].astype(F32)
+            d_buf[h, 0:HD, :] = part
+        for p in range(pairs):
+            both = jnp.concatenate([d_buf[2 * p, 0:HD, :], d_buf[2 * p + 1, 0:HD, :]], axis=0)
+            ctx[:, p * PAIR : (p + 1) * PAIR] = both.T.astype(BF16)
+        total = reduce_scatter(
+            lambda c: dot(ctx[...], w_out[:, chunk_cols(c)]).astype(BF16),
+            ysend2,
+            yrecv2,
+            zsend2,
+            zrecv2,
+            ys2_s,
+            yr2_s,
+            zs2_s,
+            zr2_s,
+        )
+        states_ref[...] = (res_ref[...].astype(F32) + total).astype(BF16)
+        for k in range(enc):
+            arrived(qg_in.at[k], qg_r.at[k])
+        for p in range(pairs):
+            at = slice(p * PAIR, (p + 1) * PAIR)
+            part = jnp.zeros((PAIR, rows), F32)
+            for k in range(enc):
+                part = part + qg_in[k, at, :].astype(F32)
+            grads_ref[:, at] = part.T.astype(BF16)
+        for k in range(enc):
+            arrived(q_ref, dq_s.at[k])
+            arrived(dg, dg_s.at[k])
+        end_gather()
+        end_scatter(ysend2, zsend2, ys2_s, zs2_s)
+
+
+def layer(slabs, groups, queries, keys_values, residual, cotangent, out_weight, kv_weight, bounds, windows):
+    rows, cols = queries.shape
+    heads = cols // HD
+    nz = groups // 2
+    enc = slabs - 1
+    width = out_weight.shape[2]
+    own = lax.dynamic_slice_in_dim(bounds, lax.axis_index("seq") * rows, rows, 1)
+    bnd = jnp.concatenate([own, bounds[:, enc * rows :]], axis=0)
+    dma = pltpu.SemaphoreType.DMA
+    blocks = lambda n: pltpu.VMEM((n, rows, cols), BF16)
+    vmem = pl.BlockSpec(memory_space=pltpu.VMEM)
+    hbm = pl.BlockSpec(memory_space=pl.ANY)
+    return pl.pallas_call(
+        functools.partial(layer_kernel, slabs, groups),
+        out_shape=(jax.ShapeDtypeStruct((rows, cols), BF16),) * 2,
+        in_specs=[vmem] * 4 + [hbm] * 2 + [vmem, pl.BlockSpec(memory_space=pltpu.SMEM)],
+        out_specs=(vmem, vmem),
+        scratch_shapes=[
+            pltpu.VMEM((cols, width), BF16),
+            pltpu.VMEM((2, width, cols), BF16),
+            pltpu.VMEM((2, rows + 2 * HALO, cols), BF16),
+            pltpu.VMEM((rows, cols), BF16),
+            blocks(nz),
+            blocks(nz),
+            blocks(nz),
+            blocks(nz),
+            blocks(nz),
+            blocks(nz),
+            blocks(nz),
+            blocks(nz),
+            blocks(nz),
+            blocks(groups),
+            pltpu.VMEM((2, rows, cols), F32),
+            blocks(2),
+            pltpu.VMEM((rows, cols), BF16),
+            pltpu.VMEM((rows, cols), BF16),
+            pltpu.VMEM((heads, rows, rows), F32),
+            pltpu.VMEM((heads, rows, rows), F32),
+            pltpu.VMEM((3, heads, rows), F32),
+            pltpu.VMEM((slabs, 3, heads, rows), F32),
+            pltpu.VMEM((2, heads, rows), F32),
+            pltpu.VMEM((cols, rows), BF16),
+            pltpu.VMEM((enc, cols, rows), BF16),
+            pltpu.VMEM((cols, rows), BF16),
+            pltpu.VMEM((enc, cols, rows), BF16),
+            blocks(2),
+            dma((2,)),
+            dma,
+            dma((2,)),
+            dma((2,)),
+        ]
+        + [dma((nz,))] * 12
+        + [
+            dma((enc,)),
+            dma,
+            dma((enc,)),
+            dma,
+            dma((enc,)),
+            dma((slabs,)),
+            dma,
+            dma((enc,)),
+            dma,
+            dma((enc,)),
+        ],
+        compiler_params=pltpu.CompilerParams(
+            collective_id=0, has_side_effects=True, vmem_limit_bytes=60 * 1024 * 1024
+        ),
+    )(queries, keys_values, residual, cotangent, out_weight, kv_weight, bnd, windows)
+
+
+def one_decoder_slab(mesh):
+    slabs, groups = mesh.shape["seq"], mesh.shape["mp"]
+    return slabs - 3 * slabs // 4 == 1 and groups % 2 == 0
+
+
 def solution(mesh):
+    body = shards
+    if one_decoder_slab(mesh):
+        body = functools.partial(layer, mesh.shape["seq"], mesh.shape["mp"])
+
     return jax.shard_map(
-        shards,
+        body,
         mesh=mesh,
         in_specs=(
             P("seq", "mp"),

time: 341 us -> 127 us (0.37)
  the two profiles are of different devices: /device:TPU:2 before, /device:TPU:16 now
where the time goes in v1:
time: 127 us
  Pallas kernels  121 us (95%)
  local copies, waits for them, and re-layouts  4.04 us (3%)
    pallas_call x1, Pallas kernels, layer(): pl.pallas_call(functools.partial(layer_kernel, slabs, groups), out_shape=...  121 us
    unnamed x2, local copies, waits for them, and re-layouts  3.34 us

profile of v1, /device:TPU:16, one launch (start us, length us, event | category | flops | bytes accessed | tf_op | source)
XLA Modules:
  0.0 126.5 jit_solution(11813423735769306483)
XLA Ops:
  0.6 0.7 constant_dynamic-slice_fusion
  1.3 0.6 pad_add_fusion.bnd_ref
  1.9 121.2 %shard_map.95 = (bf16[256,512]{1,0:T(8,128)(2,1)}, bf16[256,512]{1,0:T(8,128)(2,1)}) custom-call(bf16[256,512]{1,0:T(8,128)(2,1)} %q_ref.1, bf16[2,256,512]{2,1,0:T(8,128)(2,1)} %kv_ref.1, bf16[256,512]{1,0:T(8,128)(2,1)} %res_ref.1, bf16[256,512]{1,0:T(8,128)(2,1)} %cot_ref.1, bf16[2,512,4096]{2,1,0:T(8,128)(2,1)} %ow_ref.1, bf16[2,4096,512]{2,1,0:T(8,128)(2,1)} %kw_ref.1, ...), custom_call_target="tpu_custom_call" | custom-call | tf_op jit(solution)/shard_map/pallas_call | solution.py:728
  123.2 1.7 %copy.12 = bf16[256,512]{1,0:T(8,128)(2,1)} copy(bf16[256,512]{1,0:T(8,128)(2,1)} %get-tuple-element.6) | data formatting | bytes 524288
  124.8 1.7 %copy.13 = bf16[256,512]{1,0:T(8,128)(2,1)} copy(bf16[256,512]{1,0:T(8,128)(2,1)} %get-tuple-element.7) | data formatting | bytes 524288

commit v2 on v1

--- a/solution.py
+++ b/solution.py
@@ -202,6 +202,7 @@
 LOW = -1e30
 PAIR = 2 * HD
 HALO = 128
+BLOCKS = 2
 NT = (((1,), (1,)), ((), ()))
 
 
@@ -241,6 +242,7 @@
     zrecv2,
     gath,
     acc,
+    tot,
     kv_new,
     dq,
     dg,
@@ -266,7 +268,8 @@
     yr2_s,
     zs2_s,
     zr2_s,
-    gz_s,
+    gu_s,
+    gd_s,
     gz_r,
     gy_s,
     gy_r,
@@ -285,6 +288,7 @@
     pairs = cols // PAIR
     heads = cols // HD
     enc = slabs - 1
+    sub = rows // BLOCKS
     nz = groups // 2
     scale = HD ** (-0.5)
     s = lax.axis_index("seq")
@@ -327,20 +331,32 @@
             device_id={"seq": lax.rem(s + k, slabs), "mp": g},
             device_id_type=pl.DeviceIdType.MESH,
         )
-    for k in range(1, nz):
+
+    @pl.when(z > 0)
+    def _():
         pl.semaphore_signal(
             barrier,
             inc=1,
-            device_id={"seq": s, "mp": lax.rem(z + k, nz) * 2 + y},
+            device_id={"seq": s, "mp": (z - 1) * 2 + y},
             device_id_type=pl.DeviceIdType.MESH,
         )
+
+    @pl.when(z < nz - 1)
+    def _():
+        pl.semaphore_signal(
+            barrier,
+            inc=1,
+            device_id={"seq": s, "mp": (z + 1) * 2 + y},
+            device_id_type=pl.DeviceIdType.MESH,
+        )
+
     pl.semaphore_signal(
         barrier,
         inc=1,
         device_id={"seq": s, "mp": z * 2 + yo},
         device_id_type=pl.DeviceIdType.MESH,
     )
-    pl.semaphore_wait(barrier, slabs - 1 + nz - 1 + 1)
+    pl.semaphore_wait(barrier, slabs + jnp.where(z > 0, 1, 0) + jnp.where(z < nz - 1, 1, 0))
 
     lane = lax.broadcasted_iota(jnp.int32, (1, PAIR), 1)
     low_lane = lane < HD
@@ -356,109 +372,186 @@
     def chunk_cols(c):
         return pl.ds(pl.multiple_of(c * cols, cols), cols)
 
-    def reduce_scatter(part, ysend, yrecv, zsend, zrecv, ys, yr, zs, zr):
+    def nth(k):
+        up = nz - 1 - z
+        low = jnp.where(k < up, nz - 1 - k, k - up)
+        high = jnp.where(k < z, k, nz - 1 - (k - z))
+        return jnp.where(k == nz - 1, z, jnp.where(z < nz // 2, low, high))
+
+    def scatter_out(b, part, ysend, yrecv, ys, yr):
         def first(k, carry):
-            zt = lax.rem(z + 2 + k, nz)
-            ysend[zt] = part(zt * 2 + yo)
-            remote(ysend.at[zt], yrecv.at[zt], ys.at[zt], yr.at[zt], s, z * 2 + yo).start()
+            t = nth(k)
+            ysend[b, t] = part(b, t * 2 + yo)
+            remote(ysend.at[b, t], yrecv.at[b, t], ys.at[b, t], yr.at[b, t], s, z * 2 + yo).start()
             return carry
 
         lax.fori_loop(0, nz, first, 0)
 
+    def scatter_own(b, part):
         def own(k, carry):
-            zt = lax.rem(z + 2 + k, nz)
-            own_part[zt] = part(zt * 2 + y)
+            t = nth(k)
+            own_part[b, t] = part(b, t * 2 + y)
             return carry
 
         lax.fori_loop(0, nz, own, 0)
 
+    def scatter_in(b, yrecv, zsend, zrecv, yr, zs, zr):
+        def join(t):
+            arrived(yrecv.at[b, t], yr.at[b, t])
+            tot[...] = own_part[b, t].astype(F32) + yrecv[b, t].astype(F32)
+
+        def take(slot):
+            arrived(zrecv.at[b, slot], zr.at[b, slot])
+            tot[...] = tot[...] + zrecv[b, slot].astype(F32)
+
         def second(k, carry):
-            zt = lax.rem(z + 2 + k, nz)
-            arrived(yrecv.at[zt], yr.at[zt])
-            both = own_part[zt].astype(F32) + yrecv[zt].astype(F32)
-
-            @pl.when(zt != z)
+            t = nth(k)
+            join(t)
+
+            @pl.when((t > z) & (z > 0) | (t < z) & (z < nz - 1))
             def _():
-                zsend[zt] = both.astype(BF16)
-                remote(zsend.at[zt], zrecv.at[z], zs.at[zt], zr.at[z], s, zt * 2 + y).start()
-
-            @pl.when(zt == z)
+                take(t)
+
+            zsend[b, t] = tot[...].astype(BF16)
+
+            @pl.when(t > z)
             def _():
-                acc[0] = both
+                remote(
+                    zsend.at[b, t], zrecv.at[b, t], zs.at[b, t], zr.at[b, t], s, (z + 1) * 2 + y
+                ).start()
+
+            @pl.when(t < z)
+            def _():
+                slot = jnp.where(t == z - 1, nz, t)
+                remote(
+                    zsend.at[b, t], zrecv.at[b, slot], zs.at[b, t], zr.at[b, slot], s, (z - 1) * 2 + y
+                ).start()
 
             return carry
 
-        lax.fori_loop(0, nz, second, 0)
-
-        def third(k, carry):
-            zt = lax.rem(z + k, nz)
-            arrived(zrecv.at[zt], zr.at[zt])
-            acc[0] = acc[0] + zrecv[zt].astype(F32)
+        lax.fori_loop(0, nz - 1, second, 0)
+        join(z)
+
+        @pl.when(z > 0)
+        def _():
+            take(z)
+
+        @pl.when(z < nz - 1)
+        def _():
+            take(nz)
+
+        return tot[...]
+
+    def end_scatter(ysend, zsend, ys, zs):
+        for b in range(BLOCKS):
+            for k in range(nz):
+                arrived(ysend.at[b, k], ys.at[b, k])
+
+                @pl.when(z != k)
+                def _():
+                    arrived(zsend.at[b, k], zs.at[b, k])
+
+    def final_scatter(part, base_ref, out_ref):
+        for b in range(BLOCKS):
+            scatter_out(b, part, ysend2, yrecv2, ys2_s, yr2_s)
+        for b in range(BLOCKS):
+            scatter_own(b, part)
+        for b in range(BLOCKS):
+            at = slice(b * sub, (b + 1) * sub)
+            total = scatter_in(b, yrecv2, zsend2, zrecv2, yr2_s, zs2_s, zr2_s)
+            out_ref[at, :] = (base_ref[at, :].astype(F32) + total).astype(BF16)
+
+    def to_partner(c, t, b):
+        remote(gath.at[c, b], gath.at[c, b], gy_s.at[t, b], gy_r.at[t, b], s, z * 2 + yo).start()
+
+    def to_above(c, t, b):
+        @pl.when(z < nz - 1)
+        def _():
+            remote(
+                gath.at[c, b], gath.at[c, b], gu_s.at[t, b], gz_r.at[t, b], s, (z + 1) * 2 + y
+            ).start()
+
+    def to_below(c, t, b):
+        @pl.when(z > 0)
+        def _():
+            remote(
+                gath.at[c, b], gath.at[c, b], gd_s.at[t, b], gz_r.at[t, b], s, (z - 1) * 2 + y
+            ).start()
+
+    def gather_start(b):
+        to_above(g, z, b)
+        to_below(g, z, b)
+        to_partner(g, z, b)
+
+    def gather(use):
+        use(g)
+
+        def around(k, carry):
+            @pl.when(z >= k)
+            def _():
+                t = z - k
+                c = t * 2 + y
+                for b in range(BLOCKS):
+                    arrived(gath.at[c, b], gz_r.at[t, b])
+                    to_above(c, t, b)
+                    to_partner(c, t, b)
+
+            @pl.when(z + k < nz)
+            def _():
+                t = z + k
+                c = t * 2 + y
+                for b in range(BLOCKS):
+                    arrived(gath.at[c, b], gz_r.at[t, b])
+                    to_below(c, t, b)
+                    to_partner(c, t, b)
+
+            @pl.when(z >= k)
+            def _():
+                use((z - k) * 2 + y)
+
+            @pl.when(z + k < nz)
+            def _():
+                use((z + k) * 2 + y)
+
             return carry
 
-        lax.fori_loop(1, nz, third, 0)
-        return acc[0]
-
-    def end_scatter(ysend, zsend, ys, zs):
-        def last(k, carry):
-            arrived(ysend.at[k], ys.at[k])
+        lax.fori_loop(1, nz, around, 0)
+
+        def finish(k, carry):
+            def land(t):
+                c = t * 2 + yo
+                for b in range(BLOCKS):
+                    arrived(gath.at[c, b], gy_r.at[t, b])
+                use(c)
+
+            @pl.when(z >= k)
+            def _():
+                land(z - k)
+
+            @pl.when((k > 0) & (z + k < nz))
+            def _():
+                land(z + k)
+
             return carry
 
-        lax.fori_loop(0, nz, last, 0)
-
-        def last_z(k, carry):
-            zt = lax.rem(z + k, nz)
-            arrived(zsend.at[zt], zs.at[zt])
-            return carry
-
-        lax.fori_loop(1, nz, last_z, 0)
-
-    def gather(use):
-        remote(gath.at[g], gath.at[g], gy_s.at[z], gy_r.at[z], s, z * 2 + yo).start()
-
-        def spread(k, carry):
-            zt = lax.rem(z + 1 + k, nz)
-            remote(gath.at[g], gath.at[g], gz_s.at[zt], gz_r.at[z], s, zt * 2 + y).start()
-            return carry
-
-        lax.fori_loop(0, nz - 1, spread, 0)
-
-        def begin(k, carry):
-            zt = lax.rem(z + k, nz)
-            c = zt * 2 + y
-
-            @pl.when(k > 0)
-            def _():
-                arrived(gath.at[c], gz_r.at[zt])
-                remote(gath.at[c], gath.at[c], gy_s.at[zt], gy_r.at[zt], s, z * 2 + yo).start()
-
-            use(c)
-            return carry
-
-        lax.fori_loop(0, nz, begin, 0)
-
-        def finish(k, carry):
-            zt = lax.rem(z + k, nz)
-            c = zt * 2 + yo
-            arrived(gath.at[c], gy_r.at[zt])
-            use(c)
-            return carry
-
         lax.fori_loop(0, nz, finish, 0)
 
     def end_gather():
-        def last(k, carry):
-            arrived(gath.at[k * 2 + y], gy_s.at[k])
-            return carry
-
-        lax.fori_loop(0, nz, last, 0)
-
-        def last_z(k, carry):
-            zt = lax.rem(z + k, nz)
-            arrived(gath.at[g], gz_s.at[zt])
-            return carry
-
-        lax.fori_loop(1, nz, last_z, 0)
+        for b in range(BLOCKS):
+            for t in range(nz):
+                c = t * 2 + y
+                arrived(gath.at[c, b], gy_s.at[t, b])
+
+                @pl.when((z >= t) & (z < nz - 1))
+                def _():
+                    arrived(gath.at[c, b], gu_s.at[t, b])
+
+                @pl.when((z <= t) & (z > 0))
+                def _():
+                    arrived(gath.at[c, b], gd_s.at[t, b])
+
+    def whole_block(c):
+        return gath[c].reshape(rows, cols)
 
     def joint_stats():
         top = stat_in[0, 0]
@@ -514,49 +607,54 @@
         def _():
             arrived(kv_all.at[:, pl.ds(HALO + rows, HALO)], halo_r.at[1])
 
-        span = rows + 2 * HALO
-        key_pos = s * rows - HALO + lax.broadcasted_iota(jnp.int32, (span, 1), 0)
-        own_pos = s * rows + lax.broadcasted_iota(jnp.int32, (1, rows), 1)
-        far = jnp.abs(key_pos - own_pos)
-        in_doc = (key_pos >= bnd_ref[0:1, :]) & (key_pos <= bnd_ref[1:2, :])
-        far = jnp.where(in_doc, far, jnp.int32(1 << 20))
-
-        def local_pair(p, carry):
-            at = pair_cols(p)
-            q_pair = q_ref[:, at]
-            k_pair = kv_all[0, :, at]
-            v_t = kv_all[1, :, at].T
-            got = []
-            for i in range(2):
-                sc = dot_nt(k_pair, q_pair * lane_masks[i]) * scale
-                sc = jnp.where(far <= win_ref[p * 2 + i], sc, LOW)
-                e = jnp.exp(sc - jnp.max(sc, axis=0, keepdims=True))
-                inv = 1.0 / jnp.sum(e, axis=0, keepdims=True)
-                got.append(dot(v_t, (e * inv).astype(BF16)))
-            ctx[:, at] = jnp.where(low_row, got[0], got[1]).T.astype(BF16)
-            return carry
-
-        lax.fori_loop(0, pairs, local_pair, 0)
-        pltpu.make_async_copy(ow_ref.at[0], w_out, w_sem.at[0]).wait()
-        total = reduce_scatter(
-            lambda c: dot(ctx[...], w_out[:, chunk_cols(c)]).astype(BF16),
-            ysend,
-            yrecv,
-            zsend,
-            zrecv,
-            ys_s,
-            yr_s,
-            zs_s,
-            zr_s,
-        )
-        hidden = (res_ref[...].astype(F32) + total).astype(BF16)
-        gath[g] = hidden
-        states_ref[...] = hidden
-        acc[...] = jnp.zeros_like(acc)
+        span = sub + 2 * HALO
+
+        def attn_part(b, c):
+            return dot(ctx[b * sub : (b + 1) * sub, :], w_out[:, chunk_cols(c)]).astype(BF16)
+
+        for b in range(BLOCKS):
+            base = b * sub
+            key_pos = s * rows + base - HALO + lax.broadcasted_iota(jnp.int32, (span, 1), 0)
+            own_pos = s * rows + base + lax.broadcasted_iota(jnp.int32, (1, sub), 1)
+            far = jnp.abs(key_pos - own_pos)
+            own_at = pl.ds(pl.multiple_of(s * rows + base, sub), sub)
+            in_doc = (key_pos >= bnd_ref[0:1, own_at]) & (key_pos <= bnd_ref[1:2, own_at])
+            far_in = jnp.where(in_doc, far, jnp.int32(1 << 20))
+
+            def local_pair(p, carry):
+                at = pair_cols(p)
+                q_pair = q_ref[base : base + sub, at]
+                k_pair = kv_all[0, base : base + span, at]
+                v_t = kv_all[1, base : base + span, at].T
+                got = []
+                for i in range(2):
+                    sc = dot_nt(k_pair, q_pair * lane_masks[i]) * scale
+                    sc = jnp.where(far_in <= win_ref[p * 2 + i], sc, LOW)
+                    e = jnp.exp(sc - jnp.max(sc, axis=0, keepdims=True))
+                    inv = 1.0 / jnp.sum(e, axis=0, keepdims=True)
+                    got.append(dot(v_t, (e * inv).astype(BF16)))
+                ctx[base : base + sub, at] = jnp.where(low_row, got[0], got[1]).T.astype(BF16)
+                return carry
+
+            lax.fori_loop(0, pairs, local_pair, 0)
+            if b == 0:
+                pltpu.make_async_copy(ow_ref.at[0], w_out, w_sem.at[0]).wait()
+            scatter_out(b, attn_part, ysend, yrecv, ys_s, yr_s)
+        for b in range(BLOCKS):
+            scatter_own(b, attn_part)
+        for b in range(BLOCKS):
+            at = slice(b * sub, (b + 1) * sub)
+            total = scatter_in(b, yrecv, zsend, zrecv, yr_s, zs_s, zr_s)
+            hidden = (res_ref[at, :].astype(F32) + total).astype(BF16)
+            gath[g, b] = hidden
+            gather_start(b)
+            states_ref[at, :] = hidden
+        for i in range(2):
+            acc[i] = jnp.zeros((rows, cols), F32)
         pltpu.make_async_copy(kw_ref, w_kv, w_sem.at[1]).wait()
 
         def project(c):
-            block = gath[c]
+            block = whole_block(c)
             acc[0] = acc[0] + dot(block, w_kv[0, chunk_cols(c), :])
             acc[1] = acc[1] + dot(block, w_kv[1, chunk_cols(c), :])
 
@@ -566,7 +664,7 @@
         arrived(dg, dg_r)
 
         tok_pos = s * rows + lax.broadcasted_iota(jnp.int32, (rows, 1), 0)
-        seen = (tok_pos >= bnd_ref[2:3, :]) & (tok_pos <= bnd_ref[3:4, :])
+        seen = (tok_pos >= bnd_ref[0:1, enc * rows :]) & (tok_pos <= bnd_ref[1:2, enc * rows :])
 
         def cross_pair(p, carry):
             at = pair_cols(p)
@@ -625,20 +723,14 @@
 
         lax.fori_loop(0, pairs, grad_pair, 0)
         remote(qg_buf, qg_in.at[s], qg_s, qg_r.at[s], enc, g).start()
-        total = reduce_scatter(
-            lambda c: (
-                dot_nt(kvg[0], w_kv[0, chunk_cols(c), :]) + dot_nt(kvg[1], w_kv[1, chunk_cols(c), :])
-            ).astype(BF16),
-            ysend2,
-            yrecv2,
-            zsend2,
-            zrecv2,
-            ys2_s,
-            yr2_s,
-            zs2_s,
-            zr2_s,
-        )
-        grads_ref[...] = (cot_ref[...].astype(F32) + total).astype(BF16)
+        def grad_part(b, c):
+            at = slice(b * sub, (b + 1) * sub)
+            return (
+                dot_nt(kvg[0, at, :], w_kv[0, chunk_cols(c), :])
+                + dot_nt(kvg[1, at, :], w_kv[1, chunk_cols(c), :])
+            ).astype(BF16)
+
+        final_scatter(grad_part, cot_ref, grads_ref)
 
         @pl.when(s + 1 < enc)
         def _():
@@ -660,12 +752,14 @@
     def _():
         for k in range(enc):
             remote(q_ref, dq, dq_s.at[k], dq_r, k, g).start()
-        gath[g] = cot_ref[...]
+        for b in range(BLOCKS):
+            gath[g, b] = cot_ref[b * sub : (b + 1) * sub, :]
+            gather_start(b)
         acc[0] = jnp.zeros((rows, cols), F32)
         pltpu.make_async_copy(ow_ref.at[1], w_out, w_sem.at[0]).wait()
 
         def back(c):
-            acc[0] = acc[0] + dot_nt(gath[c], w_out[:, chunk_cols(c)])
+            acc[0] = acc[0] + dot_nt(whole_block(c), w_out[:, chunk_cols(c)])
 
         gather(back)
         dg[...] = acc[0].astype(BF16)
@@ -686,18 +780,11 @@
         for p in range(pairs):
             both = jnp.concatenate([d_buf[2 * p, 0:HD, :], d_buf[2 * p + 1, 0:HD, :]], axis=0)
             ctx[:, p * PAIR : (p + 1) * PAIR] = both.T.astype(BF16)
-        total = reduce_scatter(
-            lambda c: dot(ctx[...], w_out[:, chunk_cols(c)]).astype(BF16),
-            ysend2,
-            yrecv2,
-            zsend2,
-            zrecv2,
-            ys2_s,
-            yr2_s,
-            zs2_s,
-            zr2_s,
-        )
-        states_ref[...] = (res_ref[...].astype(F32) + total).astype(BF16)
+        final_scatter(
+            lambda b, c: dot(ctx[b * sub : (b + 1) * sub, :], w_out[:, chunk_cols(c)]).astype(BF16),
+            res_ref,
+            states_ref,
+        )
         for k in range(enc):
             arrived(qg_in.at[k], qg_r.at[k])
         for p in range(pairs):
@@ -713,19 +800,23 @@
         end_scatter(ysend2, zsend2, ys2_s, zs2_s)
 
 
+def deliver(states_in, grads_in, states_out, grads_out):
+    states_out[...] = states_in[...]
+    grads_out[...] = grads_in[...]
+
+
 def layer(slabs, groups, queries, keys_values, residual, cotangent, out_weight, kv_weight, bounds, windows):
     rows, cols = queries.shape
     heads = cols // HD
     nz = groups // 2
     enc = slabs - 1
     width = out_weight.shape[2]
-    own = lax.dynamic_slice_in_dim(bounds, lax.axis_index("seq") * rows, rows, 1)
-    bnd = jnp.concatenate([own, bounds[:, enc * rows :]], axis=0)
     dma = pltpu.SemaphoreType.DMA
     blocks = lambda n: pltpu.VMEM((n, rows, cols), BF16)
+    parts = lambda n: pltpu.VMEM((BLOCKS, n, rows // BLOCKS, cols), BF16)
     vmem = pl.BlockSpec(memory_space=pltpu.VMEM)
     hbm = pl.BlockSpec(memory_space=pl.ANY)
-    return pl.pallas_call(
+    states, grads = pl.pallas_call(
         functools.partial(layer_kernel, slabs, groups),
         out_shape=(jax.ShapeDtypeStruct((rows, cols), BF16),) * 2,
         in_specs=[vmem] * 4 + [hbm] * 2 + [vmem, pl.BlockSpec(memory_space=pltpu.SMEM)],
@@ -735,17 +826,18 @@
             pltpu.VMEM((2, width, cols), BF16),
             pltpu.VMEM((2, rows + 2 * HALO, cols), BF16),
             pltpu.VMEM((rows, cols), BF16),
-            blocks(nz),
-            blocks(nz),
-            blocks(nz),
-            blocks(nz),
-            blocks(nz),
-            blocks(nz),
-            blocks(nz),
-            blocks(nz),
-            blocks(nz),
-            blocks(groups),
+            parts(nz),
+            parts(nz),
+            parts(nz),
+            parts(nz),
+            parts(nz + 1),
+            parts(nz),
+            parts(nz),
+            parts(nz),
+            parts(nz + 1),
+            pltpu.VMEM((groups, BLOCKS, rows // BLOCKS, cols), BF16),
             pltpu.VMEM((2, rows, cols), F32),
+            pltpu.VMEM((rows // BLOCKS, cols), F32),
             blocks(2),
             pltpu.VMEM((rows, cols), BF16),
             pltpu.VMEM((rows, cols), BF16),
@@ -764,7 +856,8 @@
             dma((2,)),
             dma((2,)),
         ]
-        + [dma((nz,))] * 12
+        + [dma((BLOCKS, nz + 1))] * 8
+        + [dma((nz, BLOCKS))] * 5
         + [
             dma((enc,)),
             dma,
@@ -780,7 +873,13 @@
         compiler_params=pltpu.CompilerParams(
             collective_id=0, has_side_effects=True, vmem_limit_bytes=60 * 1024 * 1024
         ),
-    )(queries, keys_values, residual, cotangent, out_weight, kv_weight, bnd, windows)
+    )(queries, keys_values, residual, cotangent, out_weight, kv_weight, bounds, windows)
+    return pl.pallas_call(
+        deliver,
+        out_shape=(jax.ShapeDtypeStruct((rows, cols), BF16),) * 2,
+        in_specs=[vmem] * 2,
+        out_specs=(vmem, vmem),
+    )(states, grads)
 
 
 def one_decoder_slab(mesh):

time: 127 us -> 109 us (0.86)
  the two profiles are of different devices: /device:TPU:16 before, /device:TPU:2 now
where the time goes in v2:
time: 109 us; the launch traced here: 108 us
  Pallas kernels  107 us (98%)
    pallas_call x1, Pallas kernels, layer(): pl.pallas_call(functools.partial(layer_kernel, slabs, groups), out_shape=...  105 us

profile of v2, /device:TPU:2, one launch (start us, length us, event | category | flops | bytes accessed | tf_op | source)
XLA Modules:
  0.0 107.6 jit_solution(17947217406235838741)
XLA Ops:
  0.6 105.1 %shard_map.95 = (bf16[256,512]{1,0:T(8,128)(2,1)}, bf16[256,512]{1,0:T(8,128)(2,1)}) custom-call(bf16[256,512]{1,0:T(8,128)(2,1)} %q_ref.1, bf16[2,256,512]{2,1,0:T(8,128)(2,1)} %kv_ref.1, bf16[256,512]{1,0:T(8,128)(2,1)} %res_ref.1, bf16[256,512]{1,0:T(8,128)(2,1)} %cot_ref.1, bf16[2,512,4096]{2,1,0:T(8,128)(2,1)} %ow_ref.1, bf16[2,4096,512]{2,1,0:T(8,128)(2,1)} %kw_ref.1, ...), custom_call_target="tpu_custom_call" | custom-call | tf_op jit(solution)/shard_map/pallas_call | solution.py:819
  105.7 1.8 %shard_map.96 = (bf16[256,512]{1,0:T(8,128)(2,1)}, bf16[256,512]{1,0:T(8,128)(2,1)}) custom-call(bf16[256,512]{1,0:T(8,128)(2,1)} %get-tuple-element.4.states_in, bf16[256,512]{1,0:T(8,128)(2,1)} %get-tuple-element.5.grads_in), custom_call_target="tpu_custom_call" | custom-call | tf_op jit(solution)/shard_map/pallas_call | solution.py:877

commit v3 on v2

--- a/solution.py
+++ b/solution.py
@@ -243,6 +243,8 @@
     gath,
     acc,
     tot,
+    xrecv,
+    xrecv2,
     kv_new,
     dq,
     dg,
@@ -268,6 +270,10 @@
     yr2_s,
     zs2_s,
     zr2_s,
+    xr_s,
+    xr2_s,
+    gx_s,
+    gx_r,
     gu_s,
     gd_s,
     gz_r,
@@ -296,6 +302,8 @@
     z = g // 2
     y = lax.rem(g, 2)
     yo = 1 - y
+    near = z + 1 - 2 * lax.rem(z, 2)
+    tail = BLOCKS - 1
 
     def remote(src, dst, send, recv, seq, mp):
         return pltpu.make_async_remote_copy(
@@ -378,11 +386,23 @@
         high = jnp.where(k < z, k, nz - 1 - (k - z))
         return jnp.where(k == nz - 1, z, jnp.where(z < nz // 2, low, high))
 
-    def scatter_out(b, part, ysend, yrecv, ys, yr):
+    def scatter_out(b, part, ysend, yrecv, xrecv, ys, yr, xr):
         def first(k, carry):
             t = nth(k)
             ysend[b, t] = part(b, t * 2 + yo)
-            remote(ysend.at[b, t], yrecv.at[b, t], ys.at[b, t], yr.at[b, t], s, z * 2 + yo).start()
+            over = remote(ysend.at[b, t], yrecv.at[b, t], ys.at[b, t], yr.at[b, t], s, z * 2 + yo)
+            if b < tail:
+                over.start()
+            else:
+
+                @pl.when((t != near) & (t != z))
+                def _():
+                    over.start()
+
+                @pl.when(t == near)
+                def _():
+                    remote(ysend.at[b, t], xrecv, ys.at[b, t], xr, s, near * 2 + y).start()
+
             return carry
 
         lax.fori_loop(0, nz, first, 0)
@@ -395,10 +415,30 @@
 
         lax.fori_loop(0, nz, own, 0)
 
+    def scatter_late(ysend, yrecv, xrecv, ys, yr, xr):
+        arrived(xrecv, xr)
+        ysend[tail, z] = (ysend[tail, z].astype(F32) + xrecv[...].astype(F32)).astype(BF16)
+        remote(
+            ysend.at[tail, z], yrecv.at[tail, z], ys.at[tail, z], yr.at[tail, z], s, z * 2 + yo
+        ).start()
+
     def scatter_in(b, yrecv, zsend, zrecv, yr, zs, zr):
         def join(t):
-            arrived(yrecv.at[b, t], yr.at[b, t])
-            tot[...] = own_part[b, t].astype(F32) + yrecv[b, t].astype(F32)
+            def both():
+                arrived(yrecv.at[b, t], yr.at[b, t])
+                tot[...] = own_part[b, t].astype(F32) + yrecv[b, t].astype(F32)
+
+            if b < tail:
+                both()
+            else:
+
+                @pl.when(t != near)
+                def _():
+                    both()
+
+                @pl.when(t == near)
+                def _():
+                    tot[...] = own_part[b, t].astype(F32)
 
         def take(slot):
             arrived(zrecv.at[b, slot], zr.at[b, slot])
@@ -453,9 +493,10 @@
 
     def final_scatter(part, base_ref, out_ref):
         for b in range(BLOCKS):
-            scatter_out(b, part, ysend2, yrecv2, ys2_s, yr2_s)
+            scatter_out(b, part, ysend2, yrecv2, xrecv2, ys2_s, yr2_s, xr2_s)
         for b in range(BLOCKS):
             scatter_own(b, part)
+        scatter_late(ysend2, yrecv2, xrecv2, ys2_s, yr2_s, xr2_s)
         for b in range(BLOCKS):
             at = slice(b * sub, (b + 1) * sub)
             total = scatter_in(b, yrecv2, zsend2, zrecv2, yr2_s, zs2_s, zr2_s)
@@ -485,6 +526,19 @@
 
     def gather(use):
         use(g)
+        mate = z * 2 + yo
+        for b in range(BLOCKS):
+            arrived(gath.at[mate, b], gy_r.at[z, b])
+        remote(gath.at[mate, tail], gath.at[mate, tail], gx_s, gx_r, s, near * 2 + y).start()
+
+        def forward(c, t, b):
+            if b < tail:
+                to_partner(c, t, b)
+            else:
+
+                @pl.when(t != near)
+                def _():
+                    to_partner(c, t, b)
 
         def around(k, carry):
             @pl.when(z >= k)
@@ -494,7 +548,7 @@
                 for b in range(BLOCKS):
                     arrived(gath.at[c, b], gz_r.at[t, b])
                     to_above(c, t, b)
-                    to_partner(c, t, b)
+                    forward(c, t, b)
 
             @pl.when(z + k < nz)
             def _():
@@ -503,7 +557,7 @@
                 for b in range(BLOCKS):
                     arrived(gath.at[c, b], gz_r.at[t, b])
                     to_below(c, t, b)
-                    to_partner(c, t, b)
+                    forward(c, t, b)
 
             @pl.when(z >= k)
             def _():
@@ -521,7 +575,22 @@
             def land(t):
                 c = t * 2 + yo
                 for b in range(BLOCKS):
-                    arrived(gath.at[c, b], gy_r.at[t, b])
+                    if b < tail:
+
+                        @pl.when(t != z)
+                        def _():
+                            arrived(gath.at[c, b], gy_r.at[t, b])
+
+                    else:
+
+                        @pl.when((t != z) & (t != near))
+                        def _():
+                            arrived(gath.at[c, b], gy_r.at[t, b])
+
+                        @pl.when(t == near)
+                        def _():
+                            arrived(gath.at[c, b], gx_r)
+
                 use(c)
 
             @pl.when(z >= k)
@@ -537,10 +606,17 @@
         lax.fori_loop(0, nz, finish, 0)
 
     def end_gather():
+        arrived(gath.at[g, tail], gx_s)
         for b in range(BLOCKS):
             for t in range(nz):
                 c = t * 2 + y
-                arrived(gath.at[c, b], gy_s.at[t, b])
+                if b < tail:
+                    arrived(gath.at[c, b], gy_s.at[t, b])
+                else:
+
+                    @pl.when(near != t)
+                    def _():
+                        arrived(gath.at[c, b], gy_s.at[t, b])
 
                 @pl.when((z >= t) & (z < nz - 1))
                 def _():
@@ -639,9 +715,10 @@
             lax.fori_loop(0, pairs, local_pair, 0)
             if b == 0:
                 pltpu.make_async_copy(ow_ref.at[0], w_out, w_sem.at[0]).wait()
-            scatter_out(b, attn_part, ysend, yrecv, ys_s, yr_s)
+            scatter_out(b, attn_part, ysend, yrecv, xrecv, ys_s, yr_s, xr_s)
         for b in range(BLOCKS):
             scatter_own(b, attn_part)
+        scatter_late(ysend, yrecv, xrecv, ys_s, yr_s, xr_s)
         for b in range(BLOCKS):
             at = slice(b * sub, (b + 1) * sub)
             total = scatter_in(b, yrecv, zsend, zrecv, yr_s, zs_s, zr_s)
@@ -838,6 +915,8 @@
             pltpu.VMEM((groups, BLOCKS, rows // BLOCKS, cols), BF16),
             pltpu.VMEM((2, rows, cols), F32),
             pltpu.VMEM((rows // BLOCKS, cols), F32),
+            pltpu.VMEM((rows // BLOCKS, cols), BF16),
+            pltpu.VMEM((rows // BLOCKS, cols), BF16),
             blocks(2),
             pltpu.VMEM((rows, cols), BF16),
             pltpu.VMEM((rows, cols), BF16),
@@ -857,6 +936,7 @@
             dma((2,)),
         ]
         + [dma((BLOCKS, nz + 1))] * 8
+        + [dma] * 4
         + [dma((nz, BLOCKS))] * 5
         + [
             dma((enc,)),
@@ -884,7 +964,7 @@
 
 def one_decoder_slab(mesh):
     slabs, groups = mesh.shape["seq"], mesh.shape["mp"]
-    return slabs - 3 * slabs // 4 == 1 and groups % 2 == 0
+    return slabs - 3 * slabs // 4 == 1 and groups % 4 == 0
 
 
 def solution(mesh):

time: 109 us -> 114 us (1.046); the launches traced: 108 us -> 114 us
  Pallas kernels: 107 us -> 113 us
    pallas_call x1, Pallas kernels: 105 us -> 112 us  [layer(): pl.pallas_call(functools.partial(layer_kernel, slabs, groups), out_shape=...]
where the time goes in v3:
time: 114 us
  Pallas kernels  113 us (99%)
    pallas_call x1, Pallas kernels, layer(): pl.pallas_call(functools.partial(layer_kernel, slabs, groups), out_shape=...  112 us

profile of v3, /device:TPU:2, one launch (start us, length us, event | category | flops | bytes accessed | tf_op | source)
XLA Modules:
  0.0 114.1 jit_solution(2905182551105513399)
XLA Ops:
  0.6 111.6 %shard_map.95 = (bf16[256,512]{1,0:T(8,128)(2,1)}, bf16[256,512]{1,0:T(8,128)(2,1)}) custom-call(bf16[256,512]{1,0:T(8,128)(2,1)} %q_ref.1, bf16[2,256,512]{2,1,0:T(8,128)(2,1)} %kv_ref.1, bf16[256,512]{1,0:T(8,128)(2,1)} %res_ref.1, bf16[256,512]{1,0:T(8,128)(2,1)} %cot_ref.1, bf16[2,512,4096]{2,1,0:T(8,128)(2,1)} %ow_ref.1, bf16[2,4096,512]{2,1,0:T(8,128)(2,1)} %kw_ref.1, ...), custom_call_target="tpu_custom_call" | custom-call | tf_op jit(solution)/shard_map/pallas_call | solution.py:896
  112.2 1.8 %shard_map.96 = (bf16[256,512]{1,0:T(8,128)(2,1)}, bf16[256,512]{1,0:T(8,128)(2,1)}) custom-call(bf16[256,512]{1,0:T(8,128)(2,1)} %get-tuple-element.4.states_in, bf16[256,512]{1,0:T(8,128)(2,1)} %get-tuple-element.5.grads_in), custom_call_target="tpu_custom_call" | custom-call | tf_op jit(solution)/shard_map/pallas_call | solution.py:957
